TPU v7x, 128 devices: a whole 4x4x4 slice. The times are simulated.
128 devices in a mesh: body: 8 (over z, core), blk: 16 (over y, x).
Axes of the slice: x: 4, y: 4, z: 4, core: 2. Of those that a mesh axis runs over, the one named last changes fastest.
Arguments:
- state: bfloat16 [1536, 320, 128], P(('body', 'blk')), may hold values from -6 to 6
- diag_tiles: bfloat16 [1536, 320, 320], P(('body', 'blk')), may hold values from -0.125 to 0.125
- nbr_tiles: bfloat16 [1536, 4, 320, 320], P(('body', 'blk')), may hold values from -0.125 to 0.125
- nbr_list: int32 [1536, 4], P(('body', 'blk')), may hold values from 0 to 11
- donor_tiles: bfloat16 [6144, 320, 320], P(('body', 'blk')), may hold values from -0.15625 to 0.15625
- donor_src: int32 [6144, 4], P(('body', 'blk')), may hold values from 0 to 11
- donor_slot: int32 [6144], P(('body', 'blk')), may hold values from 0 to 127, as said below
- donor_recv: int32 [6144], P(('body', 'blk')), may hold values from 0 to 11
- phase: int32 [2], replicated, may hold values from 0 to 3
Outputs:
- first: bfloat16 [1536, 320, 128], P(('body', 'blk'))
- second: bfloat16 [1536, 320, 128], P(('body', 'blk'))
Inputs may be any that keep to these rules, and one draw needn't show every extreme that they name: `donor_slot`: the 48 donor tiles of one device have distinct slots, so at most 1 of them feed any one device.
All inputs are finite; a program needn't handle non-finite values.
Results may differ from a plain program's by a relative error of at most 0.0058.
Values may be sent and summed in bfloat16 or wider, within the bound.
No kernel may reach another device: no remote copies, remote signals or barrier semaphores. Data moves between devices by JAX's collectives and lax.ppermute only.
A program may use at most 192 MiB of HBM per device.

v0:
```python
import jax
import jax.numpy as jnp
from jax import lax
from jax.sharding import PartitionSpec as P


def shards(
    state, diag_tiles, nbr_tiles, nbr_list, donor_tiles, donor_src, donor_slot, donor_recv, phase
):
    blocks = state.shape[0]
    width = state.shape[1]
    columns = state.shape[2]
    groups = lax.axis_size("body")
    members = lax.axis_size("blk")
    peers = groups * members
    per_peer = max(1, 64 // peers)
    slots = peers * per_peer
    block_ids = jnp.arange(blocks, dtype=jnp.int32)

    def apply_op(vectors, column):
        inner = jnp.einsum("bij,bjv->biv", diag_tiles, vectors, preferred_element_type=jnp.float32)
        inner = inner + jnp.einsum(
            "bkij,bkjv->biv", nbr_tiles, vectors[nbr_list], preferred_element_type=jnp.float32
        )
        source = donor_src[:, column]
        partial_value = jnp.einsum(
            "eij,ejv->eiv", donor_tiles, vectors[source], preferred_element_type=jnp.float32
        ).astype(jnp.bfloat16)
        outgoing = (
            jnp.zeros((slots, width, columns), jnp.bfloat16).at[donor_slot].set(partial_value)
        )
        targets = jnp.full((slots,), blocks, jnp.int32).at[donor_slot].set(donor_recv)
        incoming, arrived = (
            lax.all_to_all(outgoing, ("body", "blk"), split_axis=0, concat_axis=0, tiled=True),
            lax.all_to_all(targets, ("body", "blk"), split_axis=0, concat_axis=0, tiled=True),
        )
        selector = (arrived[None, :] == block_ids[:, None]).astype(jnp.bfloat16)
        summed = jnp.einsum("bs,siv->biv", selector, incoming, preferred_element_type=jnp.float32)
        return (inner + summed).astype(jnp.bfloat16)

    first = apply_op(state, phase[0])
    second = apply_op(first, phase[1])
    return (first, second)


def solution(mesh):
    return jax.shard_map(
        shards,
        mesh=mesh,
        in_specs=(
            P(("body", "blk"), None, None),
            P(("body", "blk"), None, None),
            P(("body", "blk"), None, None, None),
            P(("body", "blk"), None),
            P(("body", "blk"), None, None),
            P(("body", "blk"), None),
            P(("body", "blk")),
            P(("body", "blk")),
            P(),
        ),
        out_specs=(P(("body", "blk"), None, None), P(("body", "blk"), None, None)),
        check_vma=False,
    )
```

profile of v0, /device:TPU:10, one launch (start us, length us, event | category | flops | bytes accessed | tf_op | source)
XLA Modules:
  0.0 423.1 jit_solution(9324488462124798608)
XLA Ops:
  1.5 1.0 scatter_custom_fusion
  3.2 10.4 %all-to-all-start = ((s32[128,1,1]{2,1,0:T(1,128)}), s32[128,1,1]{2,1,0:T(1,128)S(1)}, u32[]{:S(2)}, u32[]{:S(2)}) async-start(s32[128,1,1]{2,1,0:T(1,128)} %copy.28), calls=%async_computation | async-start | bytes 131072 | tf_op jit(solution)/shard_map/all_to_all | solution.py:35
  13.6 1.3 fusion.16
  19.3 4.3 %gather_fusion.1 = bf16[48,320,128]{2,1,0:T(8,128)(2,1)} fusion(bf16[12,320,128]{2,1,0:T(8,128)(2,1)} %param.9, s32[1024]{0:T(1024)S(1)} %pad_clamp_fusion.1), kind=kCustom, calls=%fused_computation.1 | custom fusion | bytes 7864512 | tf_op jit(solution)/shard_map/gather | solution.py:27
  23.6 10.5 %convert_bitcast_fusion.1 = bf16[48,320,128]{2,1,0:T(8,128)(2,1)} fusion(bf16[48,320,320]{2,1,0:T(8,128)(2,1)} %param.13, bf16[48,320,128]{2,1,0:T(8,128)(2,1)} %gather_fusion.1), kind=kOutput, calls=%fused_computation.12 | convolution fusion | flops 1260257280 | bytes 17694720 | tf_op jit(solution)/shard_map/eij,ejv->eiv/dot_general | solution.py:26
  34.1 6.4 %broadcast.32.clone = bf16[128,320,128]{2,1,0:T(8,128)(2,1)} broadcast(bf16[]{:T(256)} %constant.8.clone.1), dimensions={} | broadcast | bytes 10485762 | tf_op jit(solution)/shard_map/broadcast.9
  40.6 10.0 %scatter_fusion = bf16[128,320,128]{2,1,0:T(8,128)(2,1)} fusion(bf16[128,320,128]{2,1,0:T(8,128)(2,1)} %broadcast.32.clone, s32[48]{0:T(128)S(1)} %compare_select_fusion.3, bf16[48,320,128]{2,1,0:T(8,128)(2,1)} %convert_bitcast_fusion.1), kind=kCustom, calls=%fused_computation.5 | custom fusion | bytes 11796672 | tf_op jit(solution)/shard_map/scatter | solution.py:30
  50.6 10.8 %all-to-all-start.1 = ((bf16[128,320,128]{2,1,0:T(8,128)(2,1)}), bf16[128,320,128]{2,1,0:T(8,128)(2,1)}, u32[]{:S(2)}, u32[]{:S(2)}) async-start(bf16[128,320,128]{2,1,0:T(8,128)(2,1)} %scatter_fusion), calls=%async_computation.1 | async-start | bytes 20971520 | tf_op jit(solution)/shard_map/all_to_all | solution.py:34
  61.6 4.2 %gather_fusion = bf16[48,320,128]{2,1,0:T(8,128)(2,1)} fusion(bf16[12,320,128]{2,1,0:T(8,128)(2,1)} %param.9, s32[1024]{0:T(1024)S(1)} %pad_clamp_fusion.2), kind=kCustom, calls=%fused_computation | custom fusion | bytes 7864512 | tf_op jit(solution)/shard_map/gather | solution.py:23
  65.8 3.5 fusion.17
  69.3 2.3 reduce
  71.6 128.3 %all-to-all-done.1 = bf16[128,320,128]{2,1,0:T(8,128)(2,1)} async-done(((bf16[128,320,128]{2,1,0:T(8,128)(2,1)}), bf16[128,320,128]{2,1,0:T(8,128)(2,1)}, u32[]{:S(2)}, u32[]{:S(2)}) %all-to-all-start.1) | async-done | bytes 10485792 | tf_op jit(solution)/shard_map/all_to_all | solution.py:34
  199.9 14.5 %fusion.2 = f32[12,320,128]{2,0,1:T(8,128)S(1)} fusion(bf16[128,320,128]{2,1,0:T(8,128)(2,1)} %all-to-all-done.1, s32[128]{0:T(128)S(1)} %reduce), kind=kOutput, calls=%fused_computation.9 | convolution fusion | flops 125830656 | bytes 12452352 | tf_op jit(solution)/shard_map/bs,siv->biv/dot_general | solution.py:38
  214.5 8.8 %fusion.5 = bf16[12,320,128]{2,1,0:T(8,128)(2,1)} fusion(f32[12,320,128]{2,1,0:T(8,128)S(1)} %copy-done.3, f32[12,320,128]{2,0,1:T(8,128)S(1)} %fusion.2, bf16[12,4,320,320]{3,2,1,0:T(8,128)(2,1)} %param.11, bf16[12,4,320,128]{3,2,1,0:T(8,128)(2,1)S(1)} %bitcast.47), kind=kOutput, calls=%fused_computation.15 | convolution fusion | flops 1259765760 | bytes 18677760 | tf_op jit(solution)/shard_map/bkij,bkjv->biv/dot_general | solution.py:22
  223.3 4.3 %gather_fusion.3 = bf16[48,320,128]{2,1,0:T(8,128)(2,1)} fusion(bf16[12,320,128]{2,1,0:T(8,128)(2,1)} %fusion.5, s32[1024]{0:T(1024)S(1)} %pad_clamp_fusion), kind=kCustom, calls=%fused_computation.3 | custom fusion | bytes 7864512 | tf_op jit(solution)/shard_map/gather | solution.py:27
  227.5 10.5 %convert_bitcast_fusion = bf16[48,320,128]{2,1,0:T(8,128)(2,1)} fusion(bf16[48,320,320]{2,1,0:T(8,128)(2,1)} %param.13, bf16[48,320,128]{2,1,0:T(8,128)(2,1)} %gather_fusion.3), kind=kOutput, calls=%fused_computation.11 | convolution fusion | flops 1260257280 | bytes 17694720 | tf_op jit(solution)/shard_map/eij,ejv->eiv/dot_general | solution.py:26
  238.1 6.4 %broadcast.32 = bf16[128,320,128]{2,1,0:T(8,128)(2,1)} broadcast(bf16[]{:T(256)} %constant.8.clone.1), dimensions={} | broadcast | bytes 10485762 | tf_op jit(solution)/shard_map/broadcast.9
  244.5 10.0 %scatter_fusion.1 = bf16[128,320,128]{2,1,0:T(8,128)(2,1)} fusion(bf16[128,320,128]{2,1,0:T(8,128)(2,1)} %broadcast.32, s32[48]{0:T(128)S(1)} %compare_select_fusion.3, bf16[48,320,128]{2,1,0:T(8,128)(2,1)} %convert_bitcast_fusion), kind=kCustom, calls=%fused_computation.6 | custom fusion | bytes 11796672 | tf_op jit(solution)/shard_map/scatter | solution.py:30
  254.5 6.7 %all-to-all-start.2 = ((bf16[128,320,128]{2,1,0:T(8,128)(2,1)}), bf16[128,320,128]{2,1,0:T(8,128)(2,1)}, u32[]{:S(2)}, u32[]{:S(2)}) async-start(bf16[128,320,128]{2,1,0:T(8,128)(2,1)} %scatter_fusion.1), calls=%async_computation.2 | async-start | bytes 20971520 | tf_op jit(solution)/shard_map/all_to_all | solution.py:34
  261.1 4.2 %gather_fusion.2 = bf16[48,320,128]{2,1,0:T(8,128)(2,1)} fusion(bf16[12,320,128]{2,1,0:T(8,128)(2,1)} %fusion.5, s32[1024]{0:T(1024)S(1)} %pad_clamp_fusion.2), kind=kCustom, calls=%fused_computation.2 | custom fusion | bytes 7864512 | tf_op jit(solution)/shard_map/gather | solution.py:23
  265.4 3.5 fusion.18
  268.8 130.9 %all-to-all-done.2 = bf16[128,320,128]{2,1,0:T(8,128)(2,1)} async-done(((bf16[128,320,128]{2,1,0:T(8,128)(2,1)}), bf16[128,320,128]{2,1,0:T(8,128)(2,1)}, u32[]{:S(2)}, u32[]{:S(2)}) %all-to-all-start.2) | async-done | bytes 10485792 | tf_op jit(solution)/shard_map/all_to_all | solution.py:34
  399.7 14.3 %fusion = f32[12,320,128]{2,0,1:T(8,128)S(1)} fusion(bf16[128,320,128]{2,1,0:T(8,128)(2,1)} %all-to-all-done.2, s32[128]{0:T(128)S(1)} %reduce), kind=kOutput, calls=%fused_computation.7 | convolution fusion | flops 125830656 | bytes 12452352 | tf_op jit(solution)/shard_map/bs,siv->biv/dot_general | solution.py:38
  414.1 8.8 %fusion.6 = bf16[12,320,128]{2,1,0:T(8,128)(2,1)} fusion(f32[12,128,320]{1,2,0:T(8,128)S(1)} %copy-done.4, f32[12,320,128]{2,0,1:T(8,128)S(1)} %fusion, bf16[12,4,320,320]{3,2,1,0:T(8,128)(2,1)} %param.11, bf16[12,4,320,128]{3,2,1,0:T(8,128)(2,1)S(1)} %bitcast.48), kind=kOutput, calls=%fused_computation.17 | convolution fusion | flops 1259765760 | bytes 18677760 | tf_op jit(solution)/shard_map/bkij,bkjv->biv/dot_general | solution.py:22
  (22 shorter events, 2.6 us)
Async XLA Ops:
  0.6 65.2 %copy-start = (bf16[12,320,320]{2,1,0:T(8,128)(2,1)S(1)}, bf16[12,320,320]{2,1,0:T(8,128)(2,1)}, u32[]{:S(2)}) copy-start(bf16[12,320,320]{2,1,0:T(8,128)(2,1)} %param.10) | copy-start | bytes 7372804
  3.2 47.4 %all-to-all-start = ((s32[128,1,1]{2,1,0:T(1,128)}), s32[128,1,1]{2,1,0:T(1,128)S(1)}, u32[]{:S(2)}, u32[]{:S(2)}) async-start(s32[128,1,1]{2,1,0:T(1,128)} %copy.28), calls=%async_computation | async-start | bytes 131072 | tf_op jit(solution)/shard_map/all_to_all | solution.py:35
  50.6 10.8 %copy-start.5 = (s32[12,4]{0,1:T(4,128)S(1)}, s32[12,4]{0,1:T(4,128)}, u32[]{:S(2)}) copy-start(s32[12,4]{0,1:T(4,128)} %param.12) | copy-start | bytes 580
  50.6 149.4 %all-to-all-start.1 = ((bf16[128,320,128]{2,1,0:T(8,128)(2,1)}), bf16[128,320,128]{2,1,0:T(8,128)(2,1)}, u32[]{:S(2)}, u32[]{:S(2)}) async-start(bf16[128,320,128]{2,1,0:T(8,128)(2,1)} %scatter_fusion), calls=%async_computation.1 | async-start | bytes 20971520 | tf_op jit(solution)/shard_map/all_to_all | solution.py:34
  199.9 14.5 %copy-start.1 = (bf16[48,320,128]{2,1,0:T(8,128)(2,1)S(1)}, bf16[48,320,128]{2,1,0:T(8,128)(2,1)}, u32[]{:S(2)}) copy-start(bf16[48,320,128]{2,1,0:T(8,128)(2,1)} %gather_fusion) | copy-start | bytes 11796484
  199.9 14.5 %copy-start.3 = (f32[12,320,128]{2,1,0:T(8,128)S(1)}, f32[12,320,128]{2,1,0:T(8,128)}, u32[]{:S(2)}) copy-start(f32[12,320,128]{2,1,0:T(8,128)} %fusion.17) | copy-start | bytes 5898244
  254.5 145.2 %all-to-all-start.2 = ((bf16[128,320,128]{2,1,0:T(8,128)(2,1)}), bf16[128,320,128]{2,1,0:T(8,128)(2,1)}, u32[]{:S(2)}, u32[]{:S(2)}) async-start(bf16[128,320,128]{2,1,0:T(8,128)(2,1)} %scatter_fusion.1), calls=%async_computation.2 | async-start | bytes 20971520 | tf_op jit(solution)/shard_map/all_to_all | solution.py:34
  399.7 14.4 %copy-start.2 = (bf16[48,320,128]{2,1,0:T(8,128)(2,1)S(1)}, bf16[48,320,128]{2,1,0:T(8,128)(2,1)}, u32[]{:S(2)}) copy-start(bf16[48,320,128]{2,1,0:T(8,128)(2,1)} %gather_fusion.2) | copy-start | bytes 11796484
  399.7 14.4 %copy-start.4 = (f32[12,128,320]{1,2,0:T(8,128)S(1)}, f32[12,128,320]{1,2,0:T(8,128)}, u32[]{:S(2)}) copy-start(f32[12,128,320]{1,2,0:T(8,128)} %fusion.18) | copy-start | bytes 5898244
where the time goes:
time: 430 us; the launch traced here: 423 us
  waiting for transfers between devices  259 us (60%)
  matrix products  74.4 us (17%)
  local copies, waits for them, and re-layouts  53.1 us (12%)
  starting transfers between devices  27.9 us (6%)
  between operations  4.6 us (1%)
    all_to_all x2, waiting for transfers between devices, apply_op(): lax.all_to_all(outgoing, ('body', 'blk'), split_axis=0, concat_axis=0, ti...  259 us
    dot_general x2, matrix products, apply_op(): jnp.einsum('bs,siv->biv', selector, incoming, preferred_element_type=jnp....  28.8 us
    dot_general x2, matrix products, apply_op(): jnp.einsum('eij,ejv->eiv', donor_tiles, vectors[source], preferred_elemen...  21.1 us
    scatter x2, local copies, waits for them, and re-layouts, apply_op(): jnp.zeros((slots, width, columns), jnp.bfloat16).at[donor_slot]  19.9 us
    dot_general x2, matrix products, apply_op(): jnp.einsum('bkij,bkjv->biv', nbr_tiles, vectors[nbr_list], preferred_elem...  17.6 us
    all_to_all x2, starting transfers between devices, apply_op(): lax.all_to_all(outgoing, ('body', 'blk'), split_axis=0, concat_axis=0, ti...  17.4 us
    another operation x2, local copies, waits for them, and re-layouts  12.9 us
    all_to_all x1, starting transfers between devices, apply_op(): lax.all_to_all(targets, ('body', 'blk'), split_axis=0, concat_axis=0, til...  10.4 us
  transfers between devices with their start and end apart: 3, of which 2 were waited for; matrix products, arithmetic and copies ran while one was open for 12% of the time, Pallas kernels for 0%

commit v1 on v0

v1 whole, which is shorter than its diff:
```python
import functools

import jax
import jax.numpy as jnp
from jax import lax
from jax.experimental import pallas as pl
from jax.experimental.pallas import tpu as pltpu
from jax.sharding import PartitionSpec as P

AXES = ("body", "blk")
ANY = pl.BlockSpec(memory_space=pl.ANY)
VMEM = pl.BlockSpec(memory_space=pltpu.VMEM)
SMEM = pl.BlockSpec(memory_space=pltpu.SMEM)
LIMIT = 60 * 1024 * 1024
GROUP = 4


def dot(a, b):
    return jnp.dot(a, b, preferred_element_type=jnp.float32)


def product_kernel(source, slot, near, vectors, diag, nbr, donor, out, inner,
                   donor_buf, diag_buf, nbr_buf, made, donor_sem, diag_sem, nbr_sem, out_sem):
    count = donor.shape[0]
    blocks, fan = nbr.shape[0], nbr.shape[1]

    def donor_copy(g):
        part = pl.ds(g * GROUP, GROUP)
        return pltpu.make_async_copy(donor.at[part], donor_buf.at[part], donor_sem.at[g])

    def nbr_copy(b):
        return pltpu.make_async_copy(nbr.at[b], nbr_buf.at[b], nbr_sem.at[b])

    def out_copy(e):
        return pltpu.make_async_copy(made.at[e], out.at[slot[e]], out_sem.at[e])

    diag_copy = pltpu.make_async_copy(diag, diag_buf, diag_sem)
    for g in range(count // GROUP):
        donor_copy(g).start()
    diag_copy.start()
    for b in range(blocks):
        nbr_copy(b).start()

    @pl.loop(0, count // GROUP)
    def _(g):
        donor_copy(g).wait()
        for i in range(GROUP):
            e = g * GROUP + i
            made[e] = dot(donor_buf[e], vectors[source[e]]).astype(made.dtype)
            out_copy(e).start()

    diag_copy.wait()

    @pl.loop(0, blocks)
    def _(b):
        nbr_copy(b).wait()
        total = dot(diag_buf[b], vectors[b])
        for k in range(fan):
            total = total + dot(nbr_buf[b, k], vectors[near[b * fan + k]])
        inner[b] = total

    @pl.loop(0, count)
    def _(e):
        out_copy(e).wait()


def products(source, slot, near, vectors, diag, nbr, donor, slots):
    count = donor.shape[0]
    blocks, width, columns = vectors.shape
    return pl.pallas_call(
        product_kernel,
        out_shape=(
            jax.ShapeDtypeStruct((slots, width, columns), vectors.dtype),
            jax.ShapeDtypeStruct((blocks, width, columns), jnp.float32),
        ),
        in_specs=[SMEM, SMEM, SMEM, VMEM, ANY, ANY, ANY],
        out_specs=(ANY, VMEM),
        scratch_shapes=[
            pltpu.VMEM(donor.shape, donor.dtype),
            pltpu.VMEM(diag.shape, diag.dtype),
            pltpu.VMEM(nbr.shape, nbr.dtype),
            pltpu.VMEM((count, width, columns), vectors.dtype),
            pltpu.SemaphoreType.DMA((count // GROUP,)),
            pltpu.SemaphoreType.DMA,
            pltpu.SemaphoreType.DMA((blocks,)),
            pltpu.SemaphoreType.DMA((count,)),
        ],
        compiler_params=pltpu.CompilerParams(vmem_limit_bytes=LIMIT),
        name="products",
    )(source, slot, near, vectors, diag, nbr, donor)


def sum_kernel(target, inner, incoming, out, buf, total, sem):
    slots = incoming.shape[0]

    def copy(s):
        return pltpu.make_async_copy(incoming.at[s], buf.at[s], sem.at[s])

    @pl.loop(0, slots)
    def _(s):
        @pl.when(target[s] >= 0)
        def _():
            copy(s).start()

    total[...] = inner[...]

    @pl.loop(0, slots)
    def _(s):
        @pl.when(target[s] >= 0)
        def _():
            copy(s).wait()
            r = target[s]
            total[r] = total[r] + buf[s].astype(jnp.float32)

    out[...] = total[...].astype(out.dtype)


def summed(target, inner, incoming):
    return pl.pallas_call(
        sum_kernel,
        out_shape=jax.ShapeDtypeStruct(inner.shape, incoming.dtype),
        in_specs=[SMEM, VMEM, ANY],
        out_specs=VMEM,
        scratch_shapes=[
            pltpu.VMEM(incoming.shape, incoming.dtype),
            pltpu.VMEM(inner.shape, jnp.float32),
            pltpu.SemaphoreType.DMA((incoming.shape[0],)),
        ],
        compiler_params=pltpu.CompilerParams(vmem_limit_bytes=LIMIT),
        name="summed",
    )(target, inner, incoming)


def shards(state, diag, nbr, near, donor, donor_src, donor_slot, donor_recv, phase):
    slots = lax.axis_size("body") * lax.axis_size("blk")
    here = lax.axis_index("body") * lax.axis_size("blk") + lax.axis_index("blk")
    rows = lax.broadcasted_iota(jnp.int32, (slots, donor.shape[0]), 0)
    mine = jnp.max(jnp.where(rows == donor_slot[None, :], donor_recv[None, :], -1), axis=1)
    pattern = lax.all_gather(mine, AXES, axis=0, tiled=False)
    target = lax.dynamic_slice_in_dim(pattern, here, 1, axis=1)[:, 0]
    near = near.reshape(-1)
    columns = lax.broadcasted_iota(jnp.int32, donor_src.shape, 1)

    def apply_op(vectors, column):
        source = jnp.sum(jnp.where(columns == column, donor_src, 0), axis=1)
        outgoing, inner = products(source, donor_slot, near, vectors, diag, nbr, donor, slots)
        incoming = lax.all_to_all(outgoing, AXES, split_axis=0, concat_axis=0, tiled=True)
        return summed(target, inner, incoming)

    first = apply_op(state, phase[0])
    second = apply_op(first, phase[1])
    return first, second


def solution(mesh):
    split = P(AXES)
    return jax.shard_map(
        shards,
        mesh=mesh,
        in_specs=(split,) * 8 + (P(),),
        out_specs=(split, split),
        check_vma=False,
    )
```

time: 430 us -> 378 us (0.88); the launches traced: 423 us -> 376 us
  blocking collectives: 0 us -> 303 us
  waiting for transfers between devices: 259 us -> 0.01 us
  matrix products: 74.4 us -> 0 us
  Pallas kernels: 0 us -> 52.9 us
  local copies, waits for them, and re-layouts: 53.1 us -> 5.83 us
  starting transfers between devices: 27.9 us -> 10.8 us
    all_to_all x3 -> x1, waiting for transfers between devices: 259 us -> 0.01 us  [apply_op(): lax.all_to_all(outgoing, AXES, split_axis=0, concat_axis=0, tiled=True)]
    all_gather x0 -> x1, blocking collectives: none -> 177 us  [shards(): pattern = lax.all_gather(mine, AXES, axis=0, tiled=False)]
    all_to_all x0 -> x1, blocking collectives: none -> 126 us  [apply_op(): lax.all_to_all(outgoing, AXES, split_axis=0, concat_axis=0, tiled=True)]
    dot_general x8 -> x0, matrix products: 74.4 us -> none  [the longest x2 28.8 us: apply_op(): jnp.einsum('bs,siv->biv', selector, incoming, preferred_element_type=jnp....]
    pallas_call x0 -> x4, Pallas kernels: none -> 52.9 us  [the longest x2 37.7 us: products(): pl.pallas_call(product_kernel, out_shape=(jax.ShapeDtypeStruct((slots, wi...]
    scatter x3 -> x0, local copies, waits for them, and re-layouts: 20.9 us -> none  [the longest x2 19.9 us: apply_op(): jnp.zeros((slots, width, columns), jnp.bfloat16).at[donor_slot]]
    gather x4 -> x0, local copies, waits for them, and re-layouts: 17 us -> none  [the longest x2 8.54 us: apply_op(): vectors[source]]
    all_to_all x3 -> x1, starting transfers between devices: 27.9 us -> 10.8 us  [apply_op(): lax.all_to_all(outgoing, AXES, split_axis=0, concat_axis=0, tiled=True)]
  transfers between devices with their start and end apart: 3 -> 1, of which waited for: 2 -> 0; matrix products, arithmetic and copies ran while one was open for 12% -> 1% of each run, Pallas kernels for 0% -> 0%
where the time goes in v1:
time: 378 us; the launch traced here: 376 us
  blocking collectives  303 us (80%)
  Pallas kernels  52.9 us (14%)
  starting transfers between devices  10.8 us (3%)
  local copies, waits for them, and re-layouts  5.83 us (2%)
    all_gather x1, blocking collectives, shards(): pattern = lax.all_gather(mine, AXES, axis=0, tiled=False)  177 us
    all_to_all x1, blocking collectives, apply_op(): lax.all_to_all(outgoing, AXES, split_axis=0, concat_axis=0, tiled=True)  126 us
    pallas_call x2, Pallas kernels, products(): pl.pallas_call(product_kernel, out_shape=(jax.ShapeDtypeStruct((slots, wi...  37.7 us
    pallas_call x2, Pallas kernels, summed(): pl.pallas_call(sum_kernel, out_shape=jax.ShapeDtypeStruct(inner.shape, in...  15.2 us
    all_to_all x1, starting transfers between devices, apply_op(): lax.all_to_all(outgoing, AXES, split_axis=0, concat_axis=0, tiled=True)  10.8 us
  transfers between devices with their start and end apart: 1, of which 0 were waited for; matrix products, arithmetic and copies ran while one was open for 1% of the time, Pallas kernels for 0%

profile of v1, /device:TPU:10, one launch (start us, length us, event | category | flops | bytes accessed | tf_op | source)
XLA Modules:
  0.0 376.0 jit_solution(17749366417364308553)
XLA Ops:
  0.6 1.3 fusion
  1.9 0.8 copy.14
  2.7 0.6 reshape.9.near
  3.3 1.3 iota_compare_fusion.1
  4.6 1.3 select_reduce_fusion.1
  5.9 18.8 %products.2 = (bf16[128,320,128]{2,1,0:T(8,128)(2,1)}, f32[12,320,128]{2,1,0:T(8,128)}) custom-call(s32[48]{0:T(128)} %get-tuple-element.11.source, s32[48]{0:T(128)} %slot.3, s32[48]{0:T(128)} %reshape.9.near, bf16[12,320,128]{2,1,0:T(8,128)(2,1)} %vectors.1, bf16[12,320,320]{2,1,0:T(8,128)(2,1)} %diag.3, bf16[12,4,320,320]{3,2,1,0:T(8,128)(2,1)} %nbr.3, ...), custom_call_target="tpu_custom_call" | custom-call | tf_op jit(solution)/shard_map/products/pallas_call | solution.py:70
  24.8 0.0 copy-start
  24.8 0.0 copy-start.1
  24.8 10.8 %all-to-all-start = ((bf16[128,320,128]{2,1,0:T(8,128)(2,1)}), bf16[128,320,128]{2,1,0:T(8,128)(2,1)}, u32[]{:S(2)}, u32[]{:S(2)}) async-start(bf16[128,320,128]{2,1,0:T(8,128)(2,1)} %get-tuple-element.7), calls=%async_computation | async-start | bytes 20971520 | tf_op jit(solution)/shard_map/all_to_all | solution.py:147
  35.6 0.0 copy-done
  35.6 0.0 copy-done.1
  35.7 0.1 select_reduce_fusion
  35.7 176.9 %all-gather.1 = s32[128,1,128]{2,1,0:T(1,128)S(1)} all-gather(s32[1,1,128]{2,1,0:T(1,128)S(1)} %bitcast.3), channel_id=2, replica_groups=mesh['body'=8,'blk'=16] {'body','blk'}, dimensions={0}, use_global_device_ids=true | all-gather | bytes 66048 | tf_op jit(solution)/shard_map/all_gather | solution.py:139
  212.6 3.1 dynamic-slice_reduce_fusion.target
  215.8 0.0 all-to-all-done.incoming
  215.8 7.6 %summed.2.vectors = bf16[12,320,128]{2,1,0:T(8,128)(2,1)} custom-call(s32[128]{0:T(128)} %dynamic-slice_reduce_fusion.target, f32[12,320,128]{2,1,0:T(8,128)} %get-tuple-element.6.inner, bf16[128,320,128]{2,1,0:T(8,128)(2,1)} %all-to-all-done.incoming), custom_call_target="tpu_custom_call" | custom-call | tf_op jit(solution)/shard_map/summed/pallas_call | solution.py:119
  223.4 18.9 %products.3 = (bf16[128,320,128]{2,1,0:T(8,128)(2,1)}, f32[12,320,128]{2,1,0:T(8,128)}) custom-call(s32[48]{0:T(128)} %get-tuple-element.10.source, s32[48]{0:T(128)} %slot.3, s32[48]{0:T(128)} %reshape.9.near, bf16[12,320,128]{2,1,0:T(8,128)(2,1)} %summed.2.vectors, bf16[12,320,320]{2,1,0:T(8,128)(2,1)} %diag.3, bf16[12,4,320,320]{3,2,1,0:T(8,128)(2,1)} %nbr.3, ...), custom_call_target="tpu_custom_call" | custom-call | tf_op jit(solution)/shard_map/products/pallas_call | solution.py:70
  242.2 126.2 %all_to_all.10.incoming = bf16[128,320,128]{2,1,0:T(8,128)(2,1)} all-to-all(bf16[128,320,128]{2,1,0:T(8,128)(2,1)} %get-tuple-element.9), channel_id=1, replica_groups=mesh['body'=8,'blk'=16] {'body','blk'}, dimensions={0} | all-to-all | bytes 20971520 | tf_op jit(solution)/shard_map/all_to_all | solution.py:147
  368.5 7.6 %summed.3 = bf16[12,320,128]{2,1,0:T(8,128)(2,1)} custom-call(s32[128]{0:T(128)} %dynamic-slice_reduce_fusion.target, f32[12,320,128]{2,1,0:T(8,128)} %get-tuple-element.8.inner, bf16[128,320,128]{2,1,0:T(8,128)(2,1)} %all_to_all.10.incoming), custom_call_target="tpu_custom_call" | custom-call | tf_op jit(solution)/shard_map/summed/pallas_call | solution.py:119
Async XLA Ops:
  24.8 10.9 %copy-start = (s32[48]{0:T(128)S(1)}, s32[48]{0:T(128)}, u32[]{:S(2)}) copy-start(s32[48]{0:T(128)} %slot.3) | copy-start | bytes 580
  24.8 10.9 %copy-start.1 = (s32[48]{0:T(128)S(1)}, s32[48]{0:T(128)}, u32[]{:S(2)}) copy-start(s32[48]{0:T(128)} %param.16) | copy-start | bytes 580
  24.8 191.0 %all-to-all-start = ((bf16[128,320,128]{2,1,0:T(8,128)(2,1)}), bf16[128,320,128]{2,1,0:T(8,128)(2,1)}, u32[]{:S(2)}, u32[]{:S(2)}) async-start(bf16[128,320,128]{2,1,0:T(8,128)(2,1)} %get-tuple-element.7), calls=%async_computation | async-start | bytes 20971520 | tf_op jit(solution)/shard_map/all_to_all | solution.py:147
